TPU v7x, 32 devices: a whole 2x2x4 slice. The times are simulated.
32 devices in a mesh: group: 4 (over y, x), dev: 8 (over z, core).
Axes of the slice: x: 2, y: 2, z: 4, core: 2. Of those that a mesh axis runs over, the one named last changes fastest.
Arguments:
- q_compressed: bfloat16 [32, 1536], P('group'), may hold values from -6 to 6
- w_q_nope: bfloat16 [1536, 16384], P(None, 'dev'), may hold values from -0.15625 to 0.15625
- w_q_rope: bfloat16 [1536, 8192], P(None, 'dev'), may hold values from -0.15625 to 0.15625
- w_uk: bfloat16 [128, 128, 512], P('dev'), may hold values from -0.5 to 0.5
- w_uv: bfloat16 [128, 512, 128], P('dev'), may hold values from -0.25 to 0.25
- w_o: bfloat16 [16384, 7168], P('dev'), may hold values from -0.046875 to 0.046875
- kv_cache: bfloat16 [4, 8, 2, 2048, 576], P('group', 'dev'), may hold values from -320 to 320
- draft_kv: bfloat16 [32, 576], P('group'), may hold values from -18 to 18
- context_length: int32 [8], replicated, may hold values from 6145 to 24576
- slot_sequence: int32 [4, 8, 2], replicated, may hold values from -1 to 7, as said below
- slot_slab: int32 [4, 8, 2], replicated, may hold values from -1 to 11
Outputs:
- attn_output: float32 [32, 7168], P(('group', 'dev'))
Inputs may be any that keep to these rules, and one draw needn't show every extreme that they name: For each sequence s, slabs 0 to ceil(context_length[s] / 2048) - 1 each stand in exactly one slot of the pool, slot_sequence naming s and slot_slab the slab's number; all other slots hold -1 in both tables. The sequences' slab counts are, in some order, 4 + floor(i * 8 / 7) for i from 0 to 7. A group's slots take the slabs of its own sequences first; slabs beyond a group's 8 * 2 slots stand in free slots of other groups.
All inputs are finite; a program needn't handle non-finite values.
Results may differ from a plain program's by a relative error of at most 0.02.
The roundings to bfloat16 on the way count: a program that leaves them out, or rounds other values in their place, can miss the bound.
Values may be sent and summed in bfloat16 or wider, within the bound.
A program may use at most 128 MiB of HBM per device.

v0:
```python
import jax
import jax.numpy as jnp
from jax import lax
from jax.sharding import PartitionSpec as P

NOPE = 128
ROPE = 64
LATENT = 512
VDIM = 128
DRAFT = 4


EMPTY = -1e30


def slot_partial(row_block, slab_keys, valid_count):
    scores = lax.dot_general(
        row_block, slab_keys, (((1,), (1,)), ((), ())), preferred_element_type=jnp.float32
    )
    is_valid = jnp.arange(slab_keys.shape[0], dtype=jnp.int32) < valid_count
    masked = jnp.where(is_valid[None, :], scores, EMPTY)
    row_peak = jnp.max(masked, axis=1)
    weights = jnp.where(is_valid[None, :], jnp.exp(masked - row_peak[:, None]), 0.0)
    row_total = jnp.maximum(jnp.sum(weights, axis=1), 1.0)
    mixture = jnp.dot(
        weights.astype(jnp.bfloat16), slab_keys[:, :LATENT], preferred_element_type=jnp.float32
    )
    return (row_peak + jnp.log(row_total), mixture / row_total[:, None])


def merge_blocks(block_log, block_out, block_owner, own_log, own_out):
    owners_count = own_log.shape[0]
    matches = block_owner[None, :] == jnp.arange(owners_count, dtype=jnp.int32)[:, None]
    picked = jnp.where(matches[:, :, None, None], block_log[None], EMPTY)
    top_log = jnp.maximum(jnp.max(picked, axis=1), own_log)
    weights = jnp.where(matches[:, :, None, None], jnp.exp(picked - top_log[:, None]), 0.0)
    own_weight = jnp.exp(own_log - top_log)
    weight_sum = jnp.sum(weights, axis=1) + own_weight
    summed = jnp.einsum("sbtx,btxl->stxl", weights, block_out, precision=lax.Precision.HIGHEST)
    summed = summed + own_weight[..., None] * own_out
    return (top_log + jnp.log(weight_sum), summed / weight_sum[..., None])


def draft_partials(queries_seq, draft_rows):
    scores = jnp.einsum(
        "sthk,suk->sthu", queries_seq, draft_rows, preferred_element_type=jnp.float32
    )
    causal = jnp.arange(DRAFT)[None, :] <= jnp.arange(DRAFT)[:, None]
    masked = jnp.where(causal[None, :, None, :], scores, EMPTY)
    draft_peak = jnp.max(masked, axis=3)
    weights = jnp.where(causal[None, :, None, :], jnp.exp(masked - draft_peak[..., None]), 0.0)
    draft_total = jnp.sum(weights, axis=3)
    mixture = jnp.einsum(
        "sthu,sul->sthl",
        weights.astype(jnp.bfloat16),
        draft_rows[..., :LATENT],
        preferred_element_type=jnp.float32,
    )
    return (draft_peak + jnp.log(draft_total), mixture / draft_total[..., None])


def holder_partials(arrived, cache_slots, valid_counts):
    holder_count, slot_count, draft_count, heads_here, key_width = arrived.shape
    log_list = []
    mix_list = []
    for slot_id in range(slot_count):
        row_block = arrived[:, slot_id].reshape(holder_count * draft_count * heads_here, key_width)
        slot_log, slot_mix = slot_partial(row_block, cache_slots[slot_id], valid_counts[slot_id])
        log_list.append(slot_log.reshape(holder_count, draft_count, heads_here))
        mix_list.append(slot_mix.reshape(holder_count, draft_count, heads_here, LATENT))
    return (jnp.stack(log_list, axis=1), jnp.stack(mix_list, axis=1))


def shards(
    q_compressed,
    w_q_nope,
    w_q_rope,
    w_uk,
    w_uv,
    w_o,
    kv_cache,
    draft_kv,
    context_length,
    slot_sequence,
    slot_slab,
):
    group_count = lax.axis_size("group")
    holder_count = lax.axis_size("dev")
    group_index = lax.axis_index("group")
    holder_index = lax.axis_index("dev")
    token_count = q_compressed.shape[0]
    seq_group = token_count // DRAFT
    heads_here = w_uk.shape[0]
    key_width = LATENT + ROPE
    slab_length = kv_cache.shape[3]
    q_nope = jnp.dot(q_compressed, w_q_nope, preferred_element_type=jnp.float32).astype(
        jnp.bfloat16
    )
    q_nope = q_nope.reshape(token_count, heads_here, NOPE)
    q_rope = jnp.dot(q_compressed, w_q_rope, preferred_element_type=jnp.float32).reshape(
        token_count, heads_here, ROPE
    )
    absorbed = jnp.einsum("thn,hnl->thl", q_nope, w_uk, preferred_element_type=jnp.float32)
    queries = (jnp.concatenate([absorbed, q_rope], axis=2) * (NOPE + ROPE) ** (-0.5)).astype(
        jnp.bfloat16
    )
    queries_seq = queries.reshape(seq_group, DRAFT, heads_here, key_width)
    draft_log, draft_mix = draft_partials(
        queries_seq, draft_kv.reshape(seq_group, DRAFT, key_width)
    )
    group_table = lax.dynamic_index_in_dim(slot_sequence, group_index, 0, keepdims=False)
    own_table = lax.dynamic_index_in_dim(group_table, holder_index, 0, keepdims=False)
    own_slabs = lax.dynamic_index_in_dim(
        lax.dynamic_index_in_dim(slot_slab, group_index, 0, keepdims=False),
        holder_index,
        0,
        keepdims=False,
    )
    chosen = jnp.maximum(own_table, 0)
    valid_counts = jnp.where(own_table >= 0, context_length[chosen] - own_slabs * slab_length, 0)
    cache_slots = kv_cache[0, 0]
    pool_table = slot_sequence.reshape(group_count, -1)
    mine = group_index * seq_group + jnp.arange(seq_group, dtype=jnp.int32)
    present = jnp.any(pool_table[:, :, None] == mine[None, None, :], axis=1)
    outgoing = jnp.where(
        present[:, :, None, None, None], queries_seq[None], jnp.zeros((), jnp.bfloat16)
    )
    gathered = lax.all_to_all(outgoing, "group", split_axis=0, concat_axis=0, tiled=True)
    every_seq = gathered.reshape(group_count * seq_group, DRAFT, heads_here, key_width)
    picked = jnp.take(every_seq, jnp.maximum(group_table, 0).reshape(-1), axis=0)
    picked = picked.reshape(holder_count, -1, DRAFT, heads_here, key_width)
    arrived = lax.all_to_all(picked, "dev", split_axis=0, concat_axis=0, tiled=True)
    slot_log, slot_mix = holder_partials(arrived, cache_slots, valid_counts)
    back_log, back_mix = (
        lax.all_to_all(slot_log, "dev", split_axis=0, concat_axis=0, tiled=True),
        lax.all_to_all(slot_mix, "dev", split_axis=0, concat_axis=0, tiled=True),
    )
    seq_total = group_count * seq_group
    group_log, group_mix = merge_blocks(
        back_log.reshape(-1, DRAFT, heads_here),
        back_mix.reshape(-1, DRAFT, heads_here, LATENT),
        group_table.reshape(-1),
        jnp.full((seq_total, DRAFT, heads_here), EMPTY, jnp.float32),
        jnp.zeros((seq_total, DRAFT, heads_here, LATENT), jnp.float32),
    )
    home_log, home_mix = (
        lax.all_to_all(
            group_log.reshape(group_count, seq_group, DRAFT, heads_here),
            "group",
            split_axis=0,
            concat_axis=0,
            tiled=True,
        ),
        lax.all_to_all(
            group_mix.reshape(group_count, seq_group, DRAFT, heads_here, LATENT),
            "group",
            split_axis=0,
            concat_axis=0,
            tiled=True,
        ),
    )
    home_owner = jnp.tile(jnp.arange(seq_group, dtype=jnp.int32), group_count)
    final_log, final_mix = merge_blocks(
        home_log.reshape(-1, DRAFT, heads_here),
        home_mix.reshape(-1, DRAFT, heads_here, LATENT),
        home_owner,
        draft_log,
        draft_mix,
    )
    attended = final_mix.astype(jnp.bfloat16).reshape(token_count, heads_here, LATENT)
    head_values = jnp.einsum("thl,hlv->thv", attended, w_uv, preferred_element_type=jnp.float32)
    head_values = head_values.astype(jnp.bfloat16).reshape(token_count, heads_here * VDIM)
    return lax.psum_scatter(
        jnp.dot(head_values, w_o, preferred_element_type=jnp.float32),
        "dev",
        scatter_dimension=0,
        tiled=True,
    )


def solution(mesh):
    placed = (
        P("group", None),
        P(None, "dev"),
        P(None, "dev"),
        P("dev", None, None),
        P("dev", None, None),
        P("dev", None),
        P("group", "dev", None, None, None),
        P("group", None),
        P(),
        P(),
        P(),
    )
    return jax.shard_map(
        shards, mesh=mesh, in_specs=placed, out_specs=P(("group", "dev"), None), check_vma=False
    )
```

profile of v0, /device:TPU:1, one launch (start us, length us, event | category | flops | bytes accessed | tf_op | source)
XLA Modules:
  0.0 246.9 jit_solution(8334229183275578832)
XLA Ops:
  9.8 4.6 %convolution_bitcast_fusion = f32[8,16,512]{2,0,1:T(8,128)S(1)} fusion(bf16[16,128,512]{2,1,0:T(8,128)(2,1)} %param.14, bf16[8,1536]{1,0:T(8,128)(2,1)} %param.11, bf16[1536,2048]{1,0:T(8,128)(2,1)} %param.12), kind=kOutput, calls=%fused_computation.36 | convolution fusion | flops 67125248 | bytes 8675328 | tf_op jit(solution)/shard_map/thn,hnl->thl/dot_general | solution.py:103
  15.6 4.3 %all-to-all-start = ((bf16[4,2,4,16,576]{4,3,2,1,0:T(8,128)(2,1)}), bf16[4,2,4,16,576]{4,3,2,1,0:T(8,128)(2,1)S(1)}, u32[]{:S(2)}, u32[]{:S(2)}) async-start(bf16[4,2,4,16,576]{4,3,2,1,0:T(8,128)(2,1)} %broadcast_select_fusion.1), calls=%async_computation | async-start | bytes 1310720 | tf_op jit(solution)/shard_map/all_to_all | solution.py:128
  20.1 8.6 %all-to-all-done = bf16[4,2,4,16,576]{4,3,2,1,0:T(8,128)(2,1)S(1)} async-done(((bf16[4,2,4,16,576]{4,3,2,1,0:T(8,128)(2,1)}), bf16[4,2,4,16,576]{4,3,2,1,0:T(8,128)(2,1)S(1)}, u32[]{:S(2)}, u32[]{:S(2)}) %all-to-all-start) | async-done | bytes 589856 | tf_op jit(solution)/shard_map/all_to_all | solution.py:128
  29.6 1.3 broadcast_select_fusion
  30.8 6.3 %all-to-all-start.1 = ((bf16[8,2,4,16,576]{4,3,2,1,0:T(8,128)(2,1)}), bf16[8,2,4,16,576]{4,3,2,1,0:T(8,128)(2,1)S(1)}, u32[]{:S(2)}, u32[]{:S(2)}) async-start(bf16[8,2,4,16,576]{4,3,2,1,0:T(8,128)(2,1)} %broadcast_select_fusion), calls=%async_computation.1 | async-start | bytes 2621440 | tf_op jit(solution)/shard_map/all_to_all | solution.py:132
  40.8 5.2 %slice_bitcast_fusion.1 = (bf16[2048,576]{0,1:T(8,128)(2,1)}, bf16[2048,576]{0,1:T(8,128)(2,1)}) fusion(bf16[1,1,2,2048,576]{3,4,2,1,0:T(8,128)(2,1)} %param.17), kind=kLoop, calls=%fused_computation.11 | loop fusion | bytes 9437184 | tf_op jit(solution)/shard_map/squeeze | solution.py:68
  46.1 22.3 %all-to-all-done.1 = bf16[8,2,4,16,576]{4,3,2,1,0:T(8,128)(2,1)S(1)} async-done(((bf16[8,2,4,16,576]{4,3,2,1,0:T(8,128)(2,1)}), bf16[8,2,4,16,576]{4,3,2,1,0:T(8,128)(2,1)S(1)}, u32[]{:S(2)}, u32[]{:S(2)}) %all-to-all-start.1) | async-done | bytes 1179680 | tf_op jit(solution)/shard_map/all_to_all | solution.py:132
  68.5 3.8 %select_reduce_fusion = (f32[512]{0:T(512)S(1)}, f32[512,2048]{1,0:T(8,128)S(1)}) fusion(pred[2048]{0:T(1024)(128)(4,1)S(1)} %iota_compare_fusion, bf16[512,576]{1,0:T(8,128)(2,1)S(1)} %bitcast.102, bf16[1,1,2,2048,576]{3,4,2,1,0:T(8,128)(2,1)} %param.17), kind=kOutput, calls=%fused_computation.4 | convolution fusion | flops 1210056192 | bytes 7147520 | tf_op jit(solution)/shard_map/dot_general | solution.py:17
  73.3 1.9 select_reduce_fusion.1
  75.2 2.0 copy-done.4
  79.1 4.2 %all-to-all-start.3 = ((f32[8,1,128]{2,1,0:T(1,128)}), f32[8,1,128]{2,1,0:T(1,128)S(1)}, u32[]{:S(2)}, u32[]{:S(2)}) async-start(f32[8,1,128]{2,1,0:T(1,128)} %reshape.313), calls=%async_computation.3 | async-start | bytes 8192 | tf_op jit(solution)/shard_map/all_to_all | solution.py:135
  83.2 4.3 %fusion.40 = f32[512,512]{1,0:T(8,128)S(1)} fusion(bf16[2048,576]{0,1:T(8,128)(2,1)} %get-tuple-element.10, f32[512,2048]{1,0:T(8,128)} %copy-done.3, f32[512]{0:T(512)S(1)} %get-tuple-element.21, pred[2048]{0:T(1024)(128)(4,1)S(1)} %iota_compare_fusion, f32[512]{0:T(512)S(1)} %get-tuple-element.18), kind=kOutput, calls=%fused_computation.43 | convolution fusion | flops 1078198272 | bytes 7346176 | tf_op jit(solution)/shard_map/dot_general | solution.py:25
  88.1 1.3 fusion.35
  89.4 1.6 pad_maximum_fusion
  91.0 5.1 %all-to-all-start.2 = ((f32[8,2,4,16,512]{4,3,2,1,0:T(8,128)}), f32[8,2,4,16,512]{4,3,2,1,0:T(8,128)S(1)}, u32[]{:S(2)}, u32[]{:S(2)}) async-start(f32[8,2,4,16,512]{4,3,2,1,0:T(8,128)} %pad_maximum_fusion), calls=%async_computation.2 | async-start | bytes 4194304 | tf_op jit(solution)/shard_map/all_to_all | solution.py:136
  99.5 44.8 %all-to-all-done.2 = f32[8,2,4,16,512]{4,3,2,1,0:T(8,128)S(1)} async-done(((f32[8,2,4,16,512]{4,3,2,1,0:T(8,128)}), f32[8,2,4,16,512]{4,3,2,1,0:T(8,128)S(1)}, u32[]{:S(2)}, u32[]{:S(2)}) %all-to-all-start.2) | async-done | bytes 2097184 | tf_op jit(solution)/shard_map/all_to_all | solution.py:136
  144.2 3.2 %all-to-all-start.5 = ((f32[4,1,128]{2,1,0:T(1,128)}), f32[4,1,128]{2,1,0:T(1,128)S(1)}, u32[]{:S(2)}, u32[]{:S(2)}) async-start(f32[4,1,128]{2,1,0:T(1,128)} %reshape.315), calls=%async_computation.5 | async-start | bytes 4096 | tf_op jit(solution)/shard_map/all_to_all | solution.py:147
  147.5 2.5 %fusion.26 = f32[8,4,16,512]{3,0,2,1:T(8,128)S(1)} fusion(f32[16,4,16,512]{3,2,1,0:T(8,128)S(1)} %bitcast.97, f32[8,4,16]{0,2,1:T(8,128)S(1)} %get-tuple-element.14, f32[8,4,16]{0,2,1:T(8,128)S(1)} %get-tuple-element.13, f32[8,4,16]{0,2,1:T(8,128)S(1)} %broadcast_maximum_fusion, f32[16,4,16]{0,2,1:T(8,128)S(1)} %copy.130, ...), kind=kOutput, calls=%fused_computation.30 | convolution fusion | flops 50880512 | bytes 3156096 | tf_op jit(solution)/shard_map/sbtx,btxl->stxl/dot_general | solution.py:39
  150.6 1.5 copy.131
  152.2 3.6 %all-to-all-start.4 = ((f32[4,2,4,16,512]{4,1,3,2,0:T(2,128)}), f32[4,2,4,16,512]{4,1,3,2,0:T(2,128)S(1)}, u32[]{:S(2)}, u32[]{:S(2)}) async-start(f32[4,2,4,16,512]{4,1,3,2,0:T(2,128)} %copy.131), calls=%async_computation.4 | async-start | bytes 2097152 | tf_op jit(solution)/shard_map/all_to_all | solution.py:154
  157.4 11.5 %all-to-all-done.4 = f32[4,2,4,16,512]{4,1,3,2,0:T(2,128)S(1)} async-done(((f32[4,2,4,16,512]{4,1,3,2,0:T(2,128)}), f32[4,2,4,16,512]{4,1,3,2,0:T(2,128)S(1)}, u32[]{:S(2)}, u32[]{:S(2)}) %all-to-all-start.4) | async-done | bytes 1048608 | tf_op jit(solution)/shard_map/all_to_all | solution.py:154
  171.7 13.0 %fusion.45 = f32[8,7168]{1,0:T(8,128)} fusion(bf16[2048,7168]{1,0:T(8,128)(2,1)} %param.16, bf16[16,512,128]{2,1,0:T(8,128)(2,1)} %param.15, bf16[8,16,512]{2,1,0:T(8,128)(2,1)S(1)} %bitcast.103), kind=kOutput, calls=%fused_computation.45 | convolution fusion | flops 251674624 | bytes 31817728 | tf_op jit(solution)/shard_map/dot_general | solution.py:174
  185.4 52.4 %all-reduce.3.cloned.1.call-done = f32[8,7168]{1,0:T(8,128)} async-done(((f32[8,7168]{1,0:T(8,128)}), f32[8,7168]{1,0:T(8,128)}) %all-reduce.3.cloned.1.call-update) | async-done | bytes 229392
  237.8 2.2 constant_dynamic-slice_fusion.2
  (103 shorter events, 21.4 us)
Async XLA Ops:
  6.5 1.9 copy-start
  9.8 10.1 %copy-start.8 = (s32[4,8,2]{1,2,0:T(2,128)S(1)}, s32[4,8,2]{1,2,0:T(2,128)}, u32[]{:S(2)}) copy-start(s32[4,8,2]{1,2,0:T(2,128)} %param.20) | copy-start | bytes 772
  15.6 13.2 %all-to-all-start = ((bf16[4,2,4,16,576]{4,3,2,1,0:T(8,128)(2,1)}), bf16[4,2,4,16,576]{4,3,2,1,0:T(8,128)(2,1)S(1)}, u32[]{:S(2)}, u32[]{:S(2)}) async-start(bf16[4,2,4,16,576]{4,3,2,1,0:T(8,128)(2,1)} %broadcast_select_fusion.1), calls=%async_computation | async-start | bytes 1310720 | tf_op jit(solution)/shard_map/all_to_all | solution.py:128
  19.8 18.2 %copy-start.2 = (s32[8]{0:T(128)S(1)}, s32[8]{0:T(128)}, u32[]{:S(2)}) copy-start(s32[8]{0:T(128)} %param.19) | copy-start | bytes 100
  30.8 37.5 %all-to-all-start.1 = ((bf16[8,2,4,16,576]{4,3,2,1,0:T(8,128)(2,1)}), bf16[8,2,4,16,576]{4,3,2,1,0:T(8,128)(2,1)S(1)}, u32[]{:S(2)}, u32[]{:S(2)}) async-start(bf16[8,2,4,16,576]{4,3,2,1,0:T(8,128)(2,1)} %broadcast_select_fusion), calls=%async_computation.1 | async-start | bytes 2621440 | tf_op jit(solution)/shard_map/all_to_all | solution.py:132
  68.5 4.8 %slice-start = ((s8[4718592]{0:T(1024)(128)(4,1)}), s8[4194304]{0:T(1024)(128)(4,1)S(1)}, s32[]{:S(2)}) async-start(s8[4718592]{0:T(1024)(128)(4,1)} %bitcast.95), calls=%async_computation.7 | async-start | bytes 8388608
  68.5 4.8 %slice-start.1 = ((s8[4718592]{0:T(1024)(128)(4,1)}), s8[524288]{0:T(1024)(128)(4,1)S(1)}, s32[]{:S(2)}) async-start(s8[4718592]{0:T(1024)(128)(4,1)} %bitcast.95), calls=%async_computation.8 | async-start | bytes 1048576
  72.3 2.9 %copy-start.3 = (f32[512,2048]{1,0:T(8,128)}, f32[512,2048]{1,0:T(8,128)S(1)}, u32[]{:S(2)}) copy-start(f32[512,2048]{1,0:T(8,128)S(1)} %get-tuple-element.22) | copy-start | bytes 12582916
  75.2 2.0 copy-start.4
  79.1 12.0 %all-to-all-start.3 = ((f32[8,1,128]{2,1,0:T(1,128)}), f32[8,1,128]{2,1,0:T(1,128)S(1)}, u32[]{:S(2)}, u32[]{:S(2)}) async-start(f32[8,1,128]{2,1,0:T(1,128)} %reshape.313), calls=%async_computation.3 | async-start | bytes 8192 | tf_op jit(solution)/shard_map/all_to_all | solution.py:135
  83.2 4.3 %copy-start.5 = (f32[512,2048]{1,0:T(8,128)S(1)}, f32[512,2048]{1,0:T(8,128)}, u32[]{:S(2)}) copy-start(f32[512,2048]{1,0:T(8,128)} %copy-done.4) | copy-start | bytes 12582916
  83.2 4.8 %copy-start.6 = (bf16[2048,576]{0,1:T(8,128)(2,1)S(1)}, bf16[2048,576]{0,1:T(8,128)(2,1)}, u32[]{:S(2)}) copy-start(bf16[2048,576]{0,1:T(8,128)(2,1)} %get-tuple-element.9) | copy-start | bytes 7077892
  89.4 6.8 %copy-start.7 = (bf16[8,576]{1,0:T(8,128)(2,1)S(1)}, bf16[8,576]{1,0:T(8,128)(2,1)}, u32[]{:S(2)}) copy-start(bf16[8,576]{1,0:T(8,128)(2,1)} %param.18) | copy-start | bytes 27652
  91.0 53.2 %all-to-all-start.2 = ((f32[8,2,4,16,512]{4,3,2,1,0:T(8,128)}), f32[8,2,4,16,512]{4,3,2,1,0:T(8,128)S(1)}, u32[]{:S(2)}, u32[]{:S(2)}) async-start(f32[8,2,4,16,512]{4,3,2,1,0:T(8,128)} %pad_maximum_fusion), calls=%async_computation.2 | async-start | bytes 4194304 | tf_op jit(solution)/shard_map/all_to_all | solution.py:136
  144.2 7.9 %all-to-all-start.5 = ((f32[4,1,128]{2,1,0:T(1,128)}), f32[4,1,128]{2,1,0:T(1,128)S(1)}, u32[]{:S(2)}, u32[]{:S(2)}) async-start(f32[4,1,128]{2,1,0:T(1,128)} %reshape.315), calls=%async_computation.5 | async-start | bytes 4096 | tf_op jit(solution)/shard_map/all_to_all | solution.py:147
  152.2 16.8 %all-to-all-start.4 = ((f32[4,2,4,16,512]{4,1,3,2,0:T(2,128)}), f32[4,2,4,16,512]{4,1,3,2,0:T(2,128)S(1)}, u32[]{:S(2)}, u32[]{:S(2)}) async-start(f32[4,2,4,16,512]{4,1,3,2,0:T(2,128)} %copy.131), calls=%async_computation.4 | async-start | bytes 2097152 | tf_op jit(solution)/shard_map/all_to_all | solution.py:154
  155.7 82.1 %all-reduce.3.cloned.1.call-start = ((), (), s32[]{:S(2)}) async-start(), calls=%async_computation.6 | async-start | bytes 458752
  171.7 13.1 %copy-start.9 = (u32[32]{0:T(128)S(1)}, u32[32]{0:T(128)}, u32[]{:S(2)}) copy-start(u32[32]{0:T(128)} %constant.101) | copy-start | bytes 388
  171.7 68.4 %copy-start.1 = (bf16[1536,1024]{1,0:T(8,128)(2,1)S(1)}, bf16[1536,1024]{1,0:T(8,128)(2,1)}, u32[]{:S(2)}) copy-start(bf16[1536,1024]{1,0:T(8,128)(2,1)} %param.13) | copy-start | bytes 9437188
Sparse Core Ops, SparseCore 0:
  184.9 52.9 all-reduce.2
where the time goes:
time: 248 us; the launch traced here: 247 us
  waiting for transfers between devices  140 us (56%)
  matrix products  34.5 us (14%)
  starting transfers between devices  26.7 us (11%)
  local copies, waits for them, and re-layouts  21.6 us (9%)
  between operations  13.8 us (6%)
  other arithmetic  10.7 us (4%)
    unnamed x2, waiting for transfers between devices  52.4 us
    all_to_all x1, waiting for transfers between devices, shards(): lax.all_to_all(slot_mix, 'dev', split_axis=0, concat_axis=0, tiled=True)  44.8 us
    all_to_all x1, waiting for transfers between devices, shards(): lax.all_to_all(picked, 'dev', split_axis=0, concat_axis=0, tiled=True)  22.3 us
    dot_general x1, matrix products, shards(): jnp.dot(head_values, w_o, preferred_element_type=jnp.float32)  13 us
    all_to_all x1, waiting for transfers between devices, shards(): lax.all_to_all(group_mix.reshape(group_count, seq_group, DRAFT, heads_her...  11.5 us
    all_to_all x1, waiting for transfers between devices, shards(): lax.all_to_all(outgoing, 'group', split_axis=0, concat_axis=0, tiled=True)  8.64 us
    unnamed x31, local copies, waits for them, and re-layouts  8.4 us
    all_to_all x1, starting transfers between devices, shards(): lax.all_to_all(picked, 'dev', split_axis=0, concat_axis=0, tiled=True)  6.33 us
  transfers between devices with their start and end apart: 7, of which 5 were waited for; matrix products, arithmetic and copies ran while one was open for 11% of the time, Pallas kernels for 0%

commit v1 on v0

--- a/solution.py
+++ b/solution.py
@@ -1,6 +1,8 @@
 import jax
 import jax.numpy as jnp
 from jax import lax
+from jax.experimental import pallas as pl
+from jax.experimental.pallas import tpu as pltpu
 from jax.sharding import PartitionSpec as P
 
 NOPE = 128
@@ -11,6 +13,81 @@
 
 
 EMPTY = -1e30
+
+
+def exchange(axis, call_id, *blocks):
+    count = lax.axis_size(axis)
+    number = len(blocks)
+
+    def body(*refs):
+        sent, got = refs[:number], refs[number : 2 * number]
+        send_sems, recv_sems, local_sems = refs[2 * number :]
+        me = lax.axis_index(axis)
+        barrier = pltpu.get_barrier_semaphore()
+        for step in range(1, count):
+            pl.semaphore_signal(
+                barrier,
+                inc=1,
+                device_id={axis: lax.rem(me + step, count)},
+                device_id_type=pl.DeviceIdType.MESH,
+            )
+        pl.semaphore_wait(barrier, count - 1)
+        started = []
+        for step in range(1, count):
+            peer = lax.rem(me + step, count)
+            for which in range(number):
+                copy = pltpu.make_async_remote_copy(
+                    src_ref=sent[which].at[peer],
+                    dst_ref=got[which].at[me],
+                    send_sem=send_sems.at[which, step],
+                    recv_sem=recv_sems.at[which, step],
+                    device_id={axis: peer},
+                    device_id_type=pl.DeviceIdType.MESH,
+                )
+                copy.start()
+                started.append(copy)
+        own = []
+        for which in range(number):
+            copy = pltpu.make_async_copy(
+                sent[which].at[me], got[which].at[me], local_sems.at[which]
+            )
+            copy.start()
+            own.append(copy)
+        for copy in own:
+            copy.wait()
+        for copy in started:
+            copy.wait()
+
+    vmem = pl.BlockSpec(memory_space=pltpu.VMEM)
+    return pl.pallas_call(
+        body,
+        out_shape=tuple(jax.ShapeDtypeStruct(block.shape, block.dtype) for block in blocks),
+        in_specs=[vmem] * number,
+        out_specs=tuple([vmem] * number),
+        scratch_shapes=[
+            pltpu.SemaphoreType.DMA((number, count)),
+            pltpu.SemaphoreType.DMA((number, count)),
+            pltpu.SemaphoreType.DMA((number,)),
+        ],
+        compiler_params=pltpu.CompilerParams(
+            collective_id=call_id, has_side_effects=True, vmem_limit_bytes=32 * 1024 * 1024
+        ),
+        name="exchange_%d" % call_id,
+    )(*blocks)
+
+
+def exchange_partials(axis, call_id, block_log, block_mix):
+    count = lax.axis_size(axis)
+    flat_log = block_log.reshape(count, 1, -1)
+    width = flat_log.shape[2]
+    padded = -(-width // 128) * 128
+    flat_log = jnp.pad(flat_log, ((0, 0), (0, 0), (0, padded - width)))
+    flat_mix = block_mix.astype(jnp.bfloat16).reshape(count, -1, block_mix.shape[-1])
+    got_log, got_mix = exchange(axis, call_id, flat_log, flat_mix)
+    return (
+        got_log[:, :, :width].reshape(block_log.shape),
+        got_mix.reshape(block_mix.shape).astype(jnp.float32),
+    )
 
 
 def slot_partial(row_block, slab_keys, valid_count):
@@ -119,22 +196,16 @@
     chosen = jnp.maximum(own_table, 0)
     valid_counts = jnp.where(own_table >= 0, context_length[chosen] - own_slabs * slab_length, 0)
     cache_slots = kv_cache[0, 0]
-    pool_table = slot_sequence.reshape(group_count, -1)
-    mine = group_index * seq_group + jnp.arange(seq_group, dtype=jnp.int32)
-    present = jnp.any(pool_table[:, :, None] == mine[None, None, :], axis=1)
-    outgoing = jnp.where(
-        present[:, :, None, None, None], queries_seq[None], jnp.zeros((), jnp.bfloat16)
-    )
-    gathered = lax.all_to_all(outgoing, "group", split_axis=0, concat_axis=0, tiled=True)
+    outgoing = jnp.broadcast_to(
+        queries_seq.reshape(1, -1, key_width), (group_count, token_count * heads_here, key_width)
+    )
+    (gathered,) = exchange("group", 0, outgoing)
     every_seq = gathered.reshape(group_count * seq_group, DRAFT, heads_here, key_width)
     picked = jnp.take(every_seq, jnp.maximum(group_table, 0).reshape(-1), axis=0)
-    picked = picked.reshape(holder_count, -1, DRAFT, heads_here, key_width)
-    arrived = lax.all_to_all(picked, "dev", split_axis=0, concat_axis=0, tiled=True)
+    (arrived,) = exchange("dev", 1, picked.reshape(holder_count, -1, key_width))
+    arrived = arrived.reshape(holder_count, -1, DRAFT, heads_here, key_width)
     slot_log, slot_mix = holder_partials(arrived, cache_slots, valid_counts)
-    back_log, back_mix = (
-        lax.all_to_all(slot_log, "dev", split_axis=0, concat_axis=0, tiled=True),
-        lax.all_to_all(slot_mix, "dev", split_axis=0, concat_axis=0, tiled=True),
-    )
+    back_log, back_mix = exchange_partials("dev", 2, slot_log, slot_mix)
     seq_total = group_count * seq_group
     group_log, group_mix = merge_blocks(
         back_log.reshape(-1, DRAFT, heads_here),
@@ -143,21 +214,11 @@
         jnp.full((seq_total, DRAFT, heads_here), EMPTY, jnp.float32),
         jnp.zeros((seq_total, DRAFT, heads_here, LATENT), jnp.float32),
     )
-    home_log, home_mix = (
-        lax.all_to_all(
-            group_log.reshape(group_count, seq_group, DRAFT, heads_here),
-            "group",
-            split_axis=0,
-            concat_axis=0,
-            tiled=True,
-        ),
-        lax.all_to_all(
-            group_mix.reshape(group_count, seq_group, DRAFT, heads_here, LATENT),
-            "group",
-            split_axis=0,
-            concat_axis=0,
-            tiled=True,
-        ),
+    home_log, home_mix = exchange_partials(
+        "group",
+        3,
+        group_log.reshape(group_count, seq_group, DRAFT, heads_here),
+        group_mix.reshape(group_count, seq_group, DRAFT, heads_here, LATENT),
     )
     home_owner = jnp.tile(jnp.arange(seq_group, dtype=jnp.int32), group_count)
     final_log, final_mix = merge_blocks(
@@ -170,12 +231,11 @@
     attended = final_mix.astype(jnp.bfloat16).reshape(token_count, heads_here, LATENT)
     head_values = jnp.einsum("thl,hlv->thv", attended, w_uv, preferred_element_type=jnp.float32)
     head_values = head_values.astype(jnp.bfloat16).reshape(token_count, heads_here * VDIM)
-    return lax.psum_scatter(
-        jnp.dot(head_values, w_o, preferred_element_type=jnp.float32),
-        "dev",
-        scatter_dimension=0,
-        tiled=True,
-    )
+    partial = jnp.dot(head_values, w_o, preferred_element_type=jnp.float32)
+    (terms,) = exchange(
+        "dev", 4, partial.reshape(holder_count, token_count // holder_count, -1)
+    )
+    return jnp.sum(terms, axis=0)
 
 
 def solution(mesh):

time: 248 us -> 137 us (0.55)
  waiting for transfers between devices: 140 us -> 0 us
  Pallas kernels: 0 us -> 87.6 us
  starting transfers between devices: 26.7 us -> 0 us
  local copies, waits for them, and re-layouts: 21.6 us -> 8.12 us
  between operations: 13.8 us -> 0.35 us
  matrix products: 34.5 us -> 28.6 us
    pallas_call x0 -> x5, Pallas kernels: none -> 87.6 us  [exchange(): pl.pallas_call(body, out_shape=tuple((jax.ShapeDtypeStruct(block.shape, b...]
    all_to_all x6 -> x0, waiting for transfers between devices: 87.2 us -> none  [the longest x1 44.8 us: shards(): lax.all_to_all(slot_mix, 'dev', split_axis=0, concat_axis=0, tiled=True)]
    unnamed x2 -> x0, waiting for transfers between devices: 52.4 us -> none
    all_to_all x6 -> x0, starting transfers between devices: 26.7 us -> none  [the longest x1 6.33 us: shards(): lax.all_to_all(picked, 'dev', split_axis=0, concat_axis=0, tiled=True)]
    unnamed x31 -> x14, local copies, waits for them, and re-layouts: 8.4 us -> 0.04 us
    squeeze x1, local copies, waits for them, and re-layouts: 5.25 us -> 0.53 us  [holder_partials(): cache_slots[slot_id]]
    dot_general x2, matrix products: 5.66 us -> 2.69 us  [slot_partial(): jnp.dot(weights.astype(jnp.bfloat16), slab_keys[:, :LATENT], preferred_el...]
    reshape x3 -> x2, local copies, waits for them, and re-layouts: 2.88 us -> 0.26 us  [the longest x1 0.16 us: shards(): partial.reshape(holder_count, token_count // holder_count, -1)]
  transfers between devices with their start and end apart: 7 -> 0, of which waited for: 5 -> 0; matrix products, arithmetic and copies ran while one was open for 11% -> 0% of each run, Pallas kernels for 0% -> 0%
where the time goes in v1:
time: 137 us; the launch traced here: 136 us
  Pallas kernels  87.6 us (64%)
  matrix products  28.6 us (21%)
  other arithmetic  11.6 us (8%)
  local copies, waits for them, and re-layouts  8.12 us (6%)
    pallas_call x5, Pallas kernels, exchange(): pl.pallas_call(body, out_shape=tuple((jax.ShapeDtypeStruct(block.shape, b...  87.6 us
    dot_general x1, matrix products, shards(): partial = jnp.dot(head_values, w_o, preferred_element_type=jnp.float32)  12.4 us
    dot_general x2, matrix products, slot_partial(): lax.dot_general(row_block, slab_keys, (((1,), (1,)), ((), ())), preferred...  5.66 us
    dot_general x1, matrix products, shards(): jnp.einsum('thn,hnl->thl', q_nope, w_uk, preferred_element_type=jnp.float32)  4.62 us

profile of v1, /device:TPU:1, one launch (start us, length us, event | category | flops | bytes accessed | tf_op | source)
XLA Modules:
  0.0 136.4 jit_solution(6933192442246262112)
XLA Ops:
  0.0 1.1 multiply_reduce_fusion
  1.1 1.3 gather_fusion
  2.4 0.9 compare_reduce_fusion
  4.5 0.7 broadcast_maximum_fusion.3
  5.4 4.6 %convolution_bitcast_fusion.1 = f32[8,16,512]{2,0,1:T(8,128)S(1)} fusion(bf16[16,128,512]{2,1,0:T(8,128)(2,1)} %param.14, bf16[8,1536]{1,0:T(8,128)(2,1)} %param.11, bf16[1536,2048]{1,0:T(8,128)(2,1)} %param.12), kind=kOutput, calls=%fused_computation.34 | convolution fusion | flops 67125248 | bytes 8675328 | tf_op jit(solution)/shard_map/thn,hnl->thl/dot_general | solution.py:180
  10.0 0.9 copy.88
  11.5 1.0 fusion.39
  12.5 11.5 %exchange_0.1 = bf16[4,128,576]{2,1,0:T(8,128)(2,1)S(1)} custom-call(bf16[4,128,576]{2,1,0:T(8,128)(2,1)S(1)} %broadcast_in_dim.175.refs_0_), custom_call_target="tpu_custom_call" | custom-call | tf_op jit(solution)/shard_map/exchange_0/pallas_call | solution.py:62
  24.1 1.8 %gather_fusion.1 = bf16[16,4,16,576]{3,2,1,0:T(8,128)(2,1)} fusion(bf16[8,4,16,576]{3,2,1,0:T(8,128)(2,1)S(1)} %bitcast.82, s32[1024]{0:T(1024)S(1)} %pad_clamp_fusion), kind=kCustom, calls=%fused_computation.1 | custom fusion | bytes 2359360 | tf_op jit(solution)/shard_map/jit(_take)/gather | solution.py:204
  26.2 1.6 %broadcast_select_fusion.refs_0_ = bf16[8,128,576]{2,1,0:T(8,128)(2,1)S(1)} fusion(bf16[8,128,576]{2,1,0:T(8,128)(2,1)} %bitcast.88, pred[8,128]{1,0:T(8,128)(4,1)S(1)} %broadcast_in_dim.173), kind=kLoop, calls=%fused_computation.28 | loop fusion | flops 589824 | bytes 2360320 | tf_op jit(solution)/shard_map/jit(_take)/select_n | solution.py:204
  27.8 26.3 %exchange_1.1 = bf16[8,128,576]{2,1,0:T(8,128)(2,1)S(1)} custom-call(bf16[8,128,576]{2,1,0:T(8,128)(2,1)S(1)} %broadcast_select_fusion.refs_0_), custom_call_target="tpu_custom_call" | custom-call | tf_op jit(solution)/shard_map/exchange_1/pallas_call | solution.py:62
  54.2 3.7 %select_reduce_fusion.1 = (f32[512]{0:T(512)S(1)}, f32[512,2048]{1,0:T(8,128)S(1)}) fusion(pred[2048]{0:T(1024)(128)(4,1)S(1)} %iota_compare_fusion.1, bf16[512,576]{1,0:T(8,128)(2,1)S(1)} %bitcast.94, bf16[1,1,2,2048,576]{3,4,2,1,0:T(8,128)(2,1)} %param.17), kind=kOutput, calls=%fused_computation.5 | convolution fusion | flops 1210056192 | bytes 7147520 | tf_op jit(solution)/shard_map/dot_general | solution.py:94
  57.9 1.0 fusion.1
  59.5 1.3 divide_convert_fusion.1
  61.4 1.9 %select_reduce_fusion = (f32[512]{0:T(512)S(1)}, f32[512,2048]{1,0:T(8,128)S(1)}) fusion(pred[2048]{0:T(1024)(128)(4,1)S(1)} %iota_compare_fusion, bf16[512,576]{1,0:T(8,128)(2,1)S(1)} %bitcast.93, bf16[1,1,2,2048,576]{3,4,2,1,0:T(8,128)(2,1)S(1)} %bitcast.90), kind=kOutput, calls=%fused_computation.4 | convolution fusion | flops 1210056192 | bytes 7213056 | tf_op jit(solution)/shard_map/dot_general | solution.py:94
  63.3 1.0 fusion.3
  64.3 1.4 divide_convert_fusion
  66.1 27.7 %exchange_2.1 = (f32[8,1,128]{2,1,0:T(1,128)S(1)}, bf16[8,128,512]{2,1,0:T(8,128)(2,1)S(1)}) custom-call(f32[8,1,128]{2,1,0:T(1,128)S(1)} %reshape.319.refs_0_, bf16[8,128,512]{2,1,0:T(8,128)(2,1)S(1)} %bitcast.84), custom_call_target="tpu_custom_call" | custom-call | tf_op jit(solution)/shard_map/exchange_2/pallas_call | solution.py:62
  95.6 1.2 fusion.20
  97.3 9.3 %exchange_3.1 = (f32[4,1,128]{2,1,0:T(1,128)S(1)}, bf16[4,128,512]{2,1,0:T(8,128)(2,1)S(1)}) custom-call(f32[4,1,128]{2,1,0:T(1,128)S(1)} %log_add_fusion.1.refs_0_, bf16[4,128,512]{2,1,0:T(8,128)(2,1)S(1)} %bitcast.85), custom_call_target="tpu_custom_call" | custom-call | tf_op jit(solution)/shard_map/exchange_3/pallas_call | solution.py:62
  108.9 0.8 fusion.36
  110.1 12.4 %fusion.38 = f32[8,7168]{1,0:T(8,128)S(1)} fusion(bf16[2048,7168]{1,0:T(8,128)(2,1)} %param.16, bf16[16,512,128]{2,1,0:T(8,128)(2,1)} %param.15, bf16[8,16,512]{2,1,0:T(8,128)(2,1)S(1)} %bitcast.97), kind=kOutput, calls=%fused_computation.46 | convolution fusion | flops 251674624 | bytes 31817728 | tf_op jit(solution)/shard_map/dot_general | solution.py:234
  122.7 12.9 %exchange_4.1 = f32[8,1,7168]{2,1,0:T(1,128)S(1)} custom-call(f32[8,1,7168]{2,1,0:T(1,128)S(1)} %reshape.325.refs_0_), custom_call_target="tpu_custom_call" | custom-call | tf_op jit(solution)/shard_map/exchange_4/pallas_call | solution.py:62
  135.6 0.8 reduce_sum.64
  (76 shorter events, 9.1 us)
Async XLA Ops:
  0.0 10.9 %copy-start = (bf16[1536,1024]{1,0:T(8,128)(2,1)S(1)}, bf16[1536,1024]{1,0:T(8,128)(2,1)}, u32[]{:S(2)}) copy-start(bf16[1536,1024]{1,0:T(8,128)(2,1)} %param.13) | copy-start | bytes 9437188
  5.4 5.5 %copy-start.3 = (bf16[8,1536]{1,0:T(8,128)(2,1)S(1)}, bf16[8,1536]{1,0:T(8,128)(2,1)}, u32[]{:S(2)}) copy-start(bf16[8,1536]{1,0:T(8,128)(2,1)} %param.11) | copy-start | bytes 73732
  54.2 4.7 %slice-start = ((s8[4718592]{0:T(1024)(128)(4,1)}), s8[4194304]{0:T(1024)(128)(4,1)S(1)}, s32[]{:S(2)}) async-start(s8[4718592]{0:T(1024)(128)(4,1)} %bitcast.89), calls=%async_computation | async-start | bytes 8388608
  54.2 4.7 %slice-start.1 = ((s8[4718592]{0:T(1024)(128)(4,1)}), s8[524288]{0:T(1024)(128)(4,1)S(1)}, s32[]{:S(2)}) async-start(s8[4718592]{0:T(1024)(128)(4,1)} %bitcast.89), calls=%async_computation.1 | async-start | bytes 1048576
  95.3 12.6 %copy-start.4 = (bf16[8,576]{1,0:T(8,128)(2,1)S(1)}, bf16[8,576]{1,0:T(8,128)(2,1)}, u32[]{:S(2)}) copy-start(bf16[8,576]{1,0:T(8,128)(2,1)} %param.18) | copy-start | bytes 27652
  95.3 12.6 %copy-start.2 = (f32[8,16,512]{2,1,0:T(8,128)S(1)}, f32[8,16,512]{2,1,0:T(8,128)}, u32[]{:S(2)}) copy-start(f32[8,16,512]{2,1,0:T(8,128)} %copy.88) | copy-start | bytes 786436
  110.1 26.3 %copy-start.1 = (bf16[1536,1024]{1,0:T(8,128)(2,1)S(1)}, bf16[1536,1024]{1,0:T(8,128)(2,1)}, u32[]{:S(2)}) copy-start(bf16[1536,1024]{1,0:T(8,128)(2,1)} %param.13) | copy-start | bytes 9437188

commit v2 on v1

--- a/solution.py
+++ b/solution.py
@@ -70,7 +70,7 @@
             pltpu.SemaphoreType.DMA((number,)),
         ],
         compiler_params=pltpu.CompilerParams(
-            collective_id=call_id, has_side_effects=True, vmem_limit_bytes=32 * 1024 * 1024
+            collective_id=call_id, has_side_effects=True, vmem_limit_bytes=8 * 1024 * 1024
         ),
         name="exchange_%d" % call_id,
     )(*blocks)
@@ -90,19 +90,173 @@
     )
 
 
-def slot_partial(row_block, slab_keys, valid_count):
-    scores = lax.dot_general(
-        row_block, slab_keys, (((1,), (1,)), ((), ())), preferred_element_type=jnp.float32
-    )
-    is_valid = jnp.arange(slab_keys.shape[0], dtype=jnp.int32) < valid_count
-    masked = jnp.where(is_valid[None, :], scores, EMPTY)
-    row_peak = jnp.max(masked, axis=1)
-    weights = jnp.where(is_valid[None, :], jnp.exp(masked - row_peak[:, None]), 0.0)
-    row_total = jnp.maximum(jnp.sum(weights, axis=1), 1.0)
-    mixture = jnp.dot(
-        weights.astype(jnp.bfloat16), slab_keys[:, :LATENT], preferred_element_type=jnp.float32
-    )
-    return (row_peak + jnp.log(row_total), mixture / row_total[:, None])
+def attend_slots(call_id, every_seq, cache_slots, context_length, slot_sequence, slot_slab):
+    count = lax.axis_size("dev")
+    slot_count, slab_length, key_width = cache_slots.shape
+    seq_total, rows, _ = every_seq.shape
+    chunk = min(count, max(1, 128 // rows))
+    while count % chunk:
+        chunk -= 1
+    steps = count // chunk
+    lanes = -(-rows // 128) * 128
+    log_rows = -(-slot_count // 8) * 8
+
+    def body(
+        lengths, owners, slabs, every, cache, got_log, got_mix,
+        staged, arrived, keys, log_stage, mix_stage,
+        key_sems, send_sems, arrive_sems, back_send, back_recv,
+    ):
+        group = lax.axis_index("group")
+        me = lax.axis_index("dev")
+        barrier = pltpu.get_barrier_semaphore()
+
+        def greet(step, carry):
+            pl.semaphore_signal(
+                barrier,
+                inc=1,
+                device_id={"dev": lax.rem(me + step, count)},
+                device_id_type=pl.DeviceIdType.MESH,
+            )
+            return carry
+
+        lax.fori_loop(1, count, greet, 0)
+        for slot in range(slot_count):
+            pltpu.make_async_copy(cache.at[slot], keys.at[slot], key_sems.at[slot]).start()
+        pl.semaphore_wait(barrier, count - 1)
+
+        def row_copy(peer, source):
+            return pltpu.make_async_remote_copy(
+                src_ref=staged.at[peer],
+                dst_ref=arrived.at[source],
+                send_sem=send_sems.at[peer],
+                recv_sem=arrive_sems.at[source],
+                device_id={"dev": peer},
+                device_id_type=pl.DeviceIdType.MESH,
+            )
+
+        def back_copies(peer, source):
+            return [
+                pltpu.make_async_remote_copy(
+                    src_ref=stage.at[peer],
+                    dst_ref=target.at[source],
+                    send_sem=back_send.at[which, peer],
+                    recv_sem=back_recv.at[which, source],
+                    device_id={"dev": peer},
+                    device_id_type=pl.DeviceIdType.MESH,
+                )
+                for which, (stage, target) in enumerate([(log_stage, got_log), (mix_stage, got_mix)])
+            ]
+
+        def send_rows(step, carry):
+            peer = lax.rem(me + step, count)
+            for slot in range(slot_count):
+                owner = jnp.maximum(owners[group, peer * slot_count + slot], 0)
+                staged[peer, slot] = every[owner]
+            row_copy(peer, me).start()
+            return carry
+
+        lax.fori_loop(1, count, send_rows, 0)
+        limits = []
+        for slot in range(slot_count):
+            owner = owners[group, me * slot_count + slot]
+            arrived[me, slot] = every[jnp.maximum(owner, 0)]
+            left = lengths[jnp.maximum(owner, 0)] - slabs[group, me * slot_count + slot] * slab_length
+            limits.append(jnp.where(owner >= 0, left, 0))
+        for slot in range(slot_count):
+            pltpu.make_async_copy(cache.at[slot], keys.at[slot], key_sems.at[slot]).wait()
+
+        def one_step(step, carry):
+            first = lax.rem(me // chunk + steps - step, steps) * chunk
+            for at in range(chunk):
+                source = first + at
+
+                @pl.when(source != me)
+                def _():
+                    row_copy(source, source).wait_recv()
+
+            for slot in range(slot_count):
+                block = arrived[pl.ds(first, chunk), slot].reshape(chunk * rows, key_width)
+                scores = lax.dot_general(
+                    block, keys[slot], (((1,), (1,)), ((), ())), preferred_element_type=jnp.float32
+                )
+                place = lax.broadcasted_iota(jnp.int32, (1, slab_length), 1)
+                is_valid = place < limits[slot]
+                masked = jnp.where(is_valid, scores, EMPTY)
+                peak = jnp.max(masked, axis=1, keepdims=True)
+                weights = jnp.where(is_valid, jnp.exp(masked - peak), 0.0)
+                total = jnp.maximum(jnp.sum(weights, axis=1, keepdims=True), 1.0)
+                mixture = jnp.dot(
+                    weights.astype(jnp.bfloat16),
+                    keys[slot, :, :LATENT],
+                    preferred_element_type=jnp.float32,
+                )
+                log = jnp.broadcast_to(peak + jnp.log(total), (chunk * rows, 128))
+                mix = (mixture / total).astype(jnp.bfloat16).reshape(chunk, rows, LATENT)
+                for at in range(chunk):
+                    mix_stage[first + at, slot] = mix[at]
+                    turned = jnp.transpose(log[at * rows : (at + 1) * rows])
+                    log_stage[first + at, slot : slot + 1, :rows] = turned[:1]
+            for at in range(chunk):
+                source = first + at
+
+                @pl.when(source != me)
+                def _():
+                    for copy in back_copies(source, me):
+                        copy.start()
+
+            return carry
+
+        lax.fori_loop(0, steps, one_step, 0)
+        got_log[me] = log_stage[me]
+        got_mix[me] = mix_stage[me]
+
+        def finish(step, carry):
+            peer = lax.rem(me + step, count)
+            row_copy(peer, peer).wait_send()
+            for copy in back_copies(peer, peer):
+                copy.wait_send()
+                copy.wait_recv()
+            return carry
+
+        lax.fori_loop(1, count, finish, 0)
+
+    smem = pl.BlockSpec(memory_space=pltpu.SMEM)
+    vmem = pl.BlockSpec(memory_space=pltpu.VMEM)
+    log_shape = (count, log_rows, lanes)
+    mix_shape = (count, slot_count, rows, LATENT)
+    group_count = slot_sequence.shape[0]
+    got_log, got_mix = pl.pallas_call(
+        body,
+        out_shape=(
+            jax.ShapeDtypeStruct(log_shape, jnp.float32),
+            jax.ShapeDtypeStruct(mix_shape, jnp.bfloat16),
+        ),
+        in_specs=[smem, smem, smem, vmem, pl.BlockSpec(memory_space=pl.ANY)],
+        out_specs=(vmem, vmem),
+        scratch_shapes=[
+            pltpu.VMEM((count, slot_count, rows, key_width), jnp.bfloat16),
+            pltpu.VMEM((count, slot_count, rows, key_width), jnp.bfloat16),
+            pltpu.VMEM((slot_count, slab_length, key_width), jnp.bfloat16),
+            pltpu.VMEM(log_shape, jnp.float32),
+            pltpu.VMEM(mix_shape, jnp.bfloat16),
+            pltpu.SemaphoreType.DMA((slot_count,)),
+            pltpu.SemaphoreType.DMA((count,)),
+            pltpu.SemaphoreType.DMA((count,)),
+            pltpu.SemaphoreType.DMA((2, count)),
+            pltpu.SemaphoreType.DMA((2, count)),
+        ],
+        compiler_params=pltpu.CompilerParams(
+            collective_id=call_id, has_side_effects=True, vmem_limit_bytes=24 * 1024 * 1024
+        ),
+        name="attend_slots",
+    )(
+        context_length,
+        slot_sequence.reshape(group_count, -1),
+        slot_slab.reshape(group_count, -1),
+        every_seq,
+        cache_slots,
+    )
+    return got_log[:, :slot_count, :rows], got_mix.astype(jnp.float32)
 
 
 def merge_blocks(block_log, block_out, block_owner, own_log, own_out):
@@ -134,18 +288,6 @@
         preferred_element_type=jnp.float32,
     )
     return (draft_peak + jnp.log(draft_total), mixture / draft_total[..., None])
-
-
-def holder_partials(arrived, cache_slots, valid_counts):
-    holder_count, slot_count, draft_count, heads_here, key_width = arrived.shape
-    log_list = []
-    mix_list = []
-    for slot_id in range(slot_count):
-        row_block = arrived[:, slot_id].reshape(holder_count * draft_count * heads_here, key_width)
-        slot_log, slot_mix = slot_partial(row_block, cache_slots[slot_id], valid_counts[slot_id])
-        log_list.append(slot_log.reshape(holder_count, draft_count, heads_here))
-        mix_list.append(slot_mix.reshape(holder_count, draft_count, heads_here, LATENT))
-    return (jnp.stack(log_list, axis=1), jnp.stack(mix_list, axis=1))
 
 
 def shards(
@@ -164,12 +306,10 @@
     group_count = lax.axis_size("group")
     holder_count = lax.axis_size("dev")
     group_index = lax.axis_index("group")
-    holder_index = lax.axis_index("dev")
     token_count = q_compressed.shape[0]
     seq_group = token_count // DRAFT
     heads_here = w_uk.shape[0]
     key_width = LATENT + ROPE
-    slab_length = kv_cache.shape[3]
     q_nope = jnp.dot(q_compressed, w_q_nope, preferred_element_type=jnp.float32).astype(
         jnp.bfloat16
     )
@@ -186,26 +326,18 @@
         queries_seq, draft_kv.reshape(seq_group, DRAFT, key_width)
     )
     group_table = lax.dynamic_index_in_dim(slot_sequence, group_index, 0, keepdims=False)
-    own_table = lax.dynamic_index_in_dim(group_table, holder_index, 0, keepdims=False)
-    own_slabs = lax.dynamic_index_in_dim(
-        lax.dynamic_index_in_dim(slot_slab, group_index, 0, keepdims=False),
-        holder_index,
-        0,
-        keepdims=False,
-    )
-    chosen = jnp.maximum(own_table, 0)
-    valid_counts = jnp.where(own_table >= 0, context_length[chosen] - own_slabs * slab_length, 0)
-    cache_slots = kv_cache[0, 0]
     outgoing = jnp.broadcast_to(
         queries_seq.reshape(1, -1, key_width), (group_count, token_count * heads_here, key_width)
     )
     (gathered,) = exchange("group", 0, outgoing)
-    every_seq = gathered.reshape(group_count * seq_group, DRAFT, heads_here, key_width)
-    picked = jnp.take(every_seq, jnp.maximum(group_table, 0).reshape(-1), axis=0)
-    (arrived,) = exchange("dev", 1, picked.reshape(holder_count, -1, key_width))
-    arrived = arrived.reshape(holder_count, -1, DRAFT, heads_here, key_width)
-    slot_log, slot_mix = holder_partials(arrived, cache_slots, valid_counts)
-    back_log, back_mix = exchange_partials("dev", 2, slot_log, slot_mix)
+    back_log, back_mix = attend_slots(
+        1,
+        gathered.reshape(group_count * seq_group, DRAFT * heads_here, key_width),
+        kv_cache[0, 0],
+        context_length,
+        slot_sequence,
+        slot_slab,
+    )
     seq_total = group_count * seq_group
     group_log, group_mix = merge_blocks(
         back_log.reshape(-1, DRAFT, heads_here),

time: 137 us -> 140 us (1.022)
  local copies, waits for them, and re-layouts: 8.12 us -> 20.9 us
  other arithmetic: 11.6 us -> 2.48 us
  matrix products: 28.6 us -> 25.6 us
  Pallas kernels: 87.6 us -> 90 us
    pallas_call x0 -> x1, Pallas kernels: none -> 61.4 us  [attend_slots(): pl.pallas_call(body, out_shape=(jax.ShapeDtypeStruct(log_shape, jnp.float...]
    pallas_call x5 -> x3, Pallas kernels: 87.6 us -> 28.6 us  [exchange(): pl.pallas_call(body, out_shape=tuple((jax.ShapeDtypeStruct(block.shape, b...]
    unnamed x14 -> x19, local copies, waits for them, and re-layouts: 0.04 us -> 15.5 us
    dot_general x4 -> x0, matrix products: 8.34 us -> none  [the longest x2 5.66 us: slot_partial(): lax.dot_general(row_block, slab_keys, (((1,), (1,)), ((), ())), preferred...]
    gather x2 -> x0, local copies, waits for them, and re-layouts: 3.06 us -> none  [the longest x1 1.77 us: shards(): jnp.take(every_seq, jnp.maximum(group_table, 0).reshape(-1), axis=0)]
    dot_general x2, matrix products: 2.03 us -> 4.96 us  [merge_blocks(): jnp.einsum('sbtx,btxl->stxl', weights, block_out, precision=lax.Precision...]
    reduce_sum x2 -> x0, other arithmetic: 1.92 us -> none  [slot_partial(): row_total = jnp.maximum(jnp.sum(weights, axis=1), 1.0)]
    select_n x2 -> x0, other arithmetic: 1.58 us -> none  [the longest x1 1.57 us: shards(): jnp.take(every_seq, jnp.maximum(group_table, 0).reshape(-1), axis=0)]
where the time goes in v2:
time: 140 us; the launch traced here: 139 us
  Pallas kernels  90 us (64%)
  matrix products  25.6 us (18%)
  local copies, waits for them, and re-layouts  20.9 us (15%)
  other arithmetic  2.48 us (2%)
    pallas_call x1, Pallas kernels, attend_slots(): pl.pallas_call(body, out_shape=(jax.ShapeDtypeStruct(log_shape, jnp.float...  61.4 us
    pallas_call x3, Pallas kernels, exchange(): pl.pallas_call(body, out_shape=tuple((jax.ShapeDtypeStruct(block.shape, b...  28.6 us
    unnamed x19, local copies, waits for them, and re-layouts  15.5 us
    dot_general x1, matrix products, shards(): partial = jnp.dot(head_values, w_o, preferred_element_type=jnp.float32)  12.3 us
    dot_general x2, matrix products, merge_blocks(): jnp.einsum('sbtx,btxl->stxl', weights, block_out, precision=lax.Precision...  4.96 us
    dot_general x1, matrix products, shards(): jnp.einsum('thn,hnl->thl', q_nope, w_uk, preferred_element_type=jnp.float32)  4.6 us

profile of v2, /device:TPU:1, one launch (start us, length us, event | category | flops | bytes accessed | tf_op | source)
XLA Modules:
  0.0 139.2 jit_solution(11400458106559804056)
XLA Ops:
  0.0 0.8 constant_dynamic-slice_fusion
  1.1 0.8 copy.97
  2.0 0.8 copy.96
  2.8 0.7 reshape.204
  3.6 0.7 reshape.200
  4.3 1.3 fusion.55
  5.5 0.7 concatenate.22
  6.3 4.6 %convolution_bitcast_fusion.1 = f32[8,16,512]{2,0,1:T(8,128)S(1)} fusion(bf16[16,128,512]{2,1,0:T(8,128)(2,1)} %param.14, bf16[8,1536]{1,0:T(8,128)(2,1)S(1)} %copy-done.7, bf16[1536,2048]{1,0:T(8,128)(2,1)} %param.12), kind=kOutput, calls=%fused_computation.9 | convolution fusion | flops 67125248 | bytes 8675328 | tf_op jit(solution)/shard_map/thn,hnl->thl/dot_general | solution.py:320
  11.1 1.2 fusion.54
  12.5 11.5 %exchange_0.1 = bf16[4,128,576]{2,1,0:T(8,128)(2,1)S(1)} custom-call(bf16[4,128,576]{2,1,0:T(8,128)(2,1)S(1)} %broadcast_in_dim.118.refs_0_), custom_call_target="tpu_custom_call" | custom-call | tf_op jit(solution)/shard_map/exchange_0/pallas_call | solution.py:62
  24.0 0.8 copy-done.2
  24.9 7.7 %copy.99 = bf16[1,1,2,2048,576]{4,3,2,1,0:T(8,128)(2,1)} copy(bf16[1,1,2,2048,576]{3,4,2,1,0:T(8,128)(2,1)} %param.17) | data formatting | bytes 9437184 | tf_op args[6]
  32.6 2.5 %copy-done.1 = bf16[1,1,2,2048,576]{4,3,2,1,0:T(8,128)(2,1)S(1)} copy-done((bf16[1,1,2,2048,576]{4,3,2,1,0:T(8,128)(2,1)S(1)}, bf16[1,1,2,2048,576]{4,3,2,1,0:T(8,128)(2,1)}, u32[]{:S(2)}) %copy-start.1) | copy-done | bytes 4718616
  35.1 1.1 copy-done.3
  36.1 61.4 %attend_slots.1 = (f32[8,8,128]{2,1,0:T(8,128)S(1)}, bf16[8,2,64,512]{3,2,1,0:T(8,128)(2,1)S(1)}) custom-call(s32[8]{0:T(128)S(1)} %copy-done.4, s32[4,16]{1,0:T(4,128)S(1)} %copy.100.owners, s32[4,16]{1,0:T(4,128)S(1)} %copy.101.slabs, bf16[8,64,576]{2,1,0:T(8,128)(2,1)S(1)} %bitcast.61, bf16[2,2048,576]{2,1,0:T(8,128)(2,1)S(1)} %bitcast.60), custom_call_target="tpu_custom_call" | custom-call | tf_op jit(solution)/shard_map/attend_slots/pallas_call | solution.py:228
  97.6 1.0 copy-done.5
  99.5 2.4 %fusion.2 = bf16[8,4,16,512]{3,0,2,1:T(8,128)(2,1)S(1)} fusion(bf16[16,4,16,512]{3,2,1,0:T(8,128)(2,1)} %bitcast.63, f32[8,4,16]{0,2,1:T(8,128)S(1)} %get-tuple-element.16, f32[8,4,16]{0,2,1:T(8,128)S(1)} %get-tuple-element.15, f32[8,4,16]{0,2,1:T(8,128)S(1)} %broadcast_maximum_fusion, f32[16,4,16]{0,2,1:T(8,128)S(1)} %copy.102, ...), kind=kOutput, calls=%fused_computation.4 | convolution fusion | flops 51142656 | bytes 1583232 | tf_op jit(solution)/shard_map/sbtx,btxl->stxl/dot_general | solution.py:270
  102.1 9.0 %exchange_3.1 = (f32[4,1,128]{2,1,0:T(1,128)S(1)}, bf16[4,128,512]{2,1,0:T(8,128)(2,1)S(1)}) custom-call(f32[4,1,128]{2,1,0:T(1,128)S(1)} %log_add_fusion.1.refs_0_, bf16[4,128,512]{2,1,0:T(8,128)(2,1)S(1)} %bitcast.62), custom_call_target="tpu_custom_call" | custom-call | tf_op jit(solution)/shard_map/exchange_3/pallas_call | solution.py:62
  111.1 0.8 copy-done.6
  113.6 2.6 %fusion.10 = f32[4,16,512,2]{2,3,1,0:T(2,128)} fusion(bf16[8,4,16,512]{3,2,1,0:T(8,128)(2,1)} %bitcast.64, pred[2,8]{1,0:T(4,128)(4,1)S(1)} %iota_compare_fusion.2, f32[2,4,16]{0,2,1:T(8,128)S(1)} %copy.110, f32[8,4,16]{0,2,1:T(8,128)S(1)} %copy.107), kind=kOutput, calls=%fused_computation.16 | convolution fusion | flops 6294528 | bytes 789008 | tf_op jit(solution)/shard_map/sbtx,btxl->stxl/dot_general | solution.py:270
  116.5 1.3 fusion.6
  117.8 12.3 %fusion.12 = f32[8,7168]{1,0:T(8,128)S(1)} fusion(bf16[2048,7168]{1,0:T(8,128)(2,1)} %param.16, bf16[16,512,128]{2,1,0:T(8,128)(2,1)} %param.15, bf16[8,16,512]{2,1,0:T(8,128)(2,1)S(1)} %bitcast.67), kind=kOutput, calls=%fused_computation.18 | convolution fusion | flops 251674624 | bytes 31817728 | tf_op jit(solution)/shard_map/dot_general | solution.py:366
  130.3 8.1 %exchange_4.1 = f32[8,1,7168]{2,1,0:T(1,128)S(1)} custom-call(f32[8,1,7168]{2,1,0:T(1,128)S(1)} %reshape.203.refs_0_), custom_call_target="tpu_custom_call" | custom-call | tf_op jit(solution)/shard_map/exchange_4/pallas_call | solution.py:62
  138.4 0.8 reduce_sum.44
  (50 shorter events, 4.2 us)
Async XLA Ops:
  0.0 4.3 %copy-start = (bf16[1536,1024]{1,0:T(8,128)(2,1)S(1)}, bf16[1536,1024]{1,0:T(8,128)(2,1)}, u32[]{:S(2)}) copy-start(bf16[1536,1024]{1,0:T(8,128)(2,1)} %param.13) | copy-start | bytes 9437188
  0.0 6.3 %copy-start.7 = (bf16[8,1536]{1,0:T(8,128)(2,1)S(1)}, bf16[8,1536]{1,0:T(8,128)(2,1)}, u32[]{:S(2)}) copy-start(bf16[8,1536]{1,0:T(8,128)(2,1)} %param.11) | copy-start | bytes 73732
  24.0 0.9 copy-start.2
  24.9 7.7 %copy-start.4 = (s32[8]{0:T(128)S(1)}, s32[8]{0:T(128)}, u32[]{:S(2)}) copy-start(s32[8]{0:T(128)} %lengths.1) | copy-start | bytes 100
  32.6 2.5 %copy-start.1 = (bf16[1,1,2,2048,576]{4,3,2,1,0:T(8,128)(2,1)S(1)}, bf16[1,1,2,2048,576]{4,3,2,1,0:T(8,128)(2,1)}, u32[]{:S(2)}) copy-start(bf16[1,1,2,2048,576]{4,3,2,1,0:T(8,128)(2,1)} %copy.99) | copy-start | bytes 14155780
  35.1 1.1 copy-start.3
  97.5 1.0 copy-start.5
  111.1 0.8 copy-start.6

commit v3 on v2

--- a/solution.py
+++ b/solution.py
@@ -92,7 +92,7 @@
 
 def attend_slots(call_id, every_seq, cache_slots, context_length, slot_sequence, slot_slab):
     count = lax.axis_size("dev")
-    slot_count, slab_length, key_width = cache_slots.shape
+    slot_count, key_width, slab_length = cache_slots.shape
     seq_total, rows, _ = every_seq.shape
     chunk = min(count, max(1, 128 // rows))
     while count % chunk:
@@ -150,7 +150,7 @@
         def send_rows(step, carry):
             peer = lax.rem(me + step, count)
             for slot in range(slot_count):
-                owner = jnp.maximum(owners[group, peer * slot_count + slot], 0)
+                owner = jnp.maximum(owners[group, peer, slot], 0)
                 staged[peer, slot] = every[owner]
             row_copy(peer, me).start()
             return carry
@@ -158,9 +158,9 @@
         lax.fori_loop(1, count, send_rows, 0)
         limits = []
         for slot in range(slot_count):
-            owner = owners[group, me * slot_count + slot]
+            owner = owners[group, me, slot]
             arrived[me, slot] = every[jnp.maximum(owner, 0)]
-            left = lengths[jnp.maximum(owner, 0)] - slabs[group, me * slot_count + slot] * slab_length
+            left = lengths[jnp.maximum(owner, 0)] - slabs[group, me, slot] * slab_length
             limits.append(jnp.where(owner >= 0, left, 0))
         for slot in range(slot_count):
             pltpu.make_async_copy(cache.at[slot], keys.at[slot], key_sems.at[slot]).wait()
@@ -177,7 +177,7 @@
             for slot in range(slot_count):
                 block = arrived[pl.ds(first, chunk), slot].reshape(chunk * rows, key_width)
                 scores = lax.dot_general(
-                    block, keys[slot], (((1,), (1,)), ((), ())), preferred_element_type=jnp.float32
+                    block, keys[slot], (((1,), (0,)), ((), ())), preferred_element_type=jnp.float32
                 )
                 place = lax.broadcasted_iota(jnp.int32, (1, slab_length), 1)
                 is_valid = place < limits[slot]
@@ -185,9 +185,10 @@
                 peak = jnp.max(masked, axis=1, keepdims=True)
                 weights = jnp.where(is_valid, jnp.exp(masked - peak), 0.0)
                 total = jnp.maximum(jnp.sum(weights, axis=1, keepdims=True), 1.0)
-                mixture = jnp.dot(
+                mixture = lax.dot_general(
                     weights.astype(jnp.bfloat16),
-                    keys[slot, :, :LATENT],
+                    keys[slot, :LATENT],
+                    (((1,), (1,)), ((), ())),
                     preferred_element_type=jnp.float32,
                 )
                 log = jnp.broadcast_to(peak + jnp.log(total), (chunk * rows, 128))
@@ -224,7 +225,6 @@
     vmem = pl.BlockSpec(memory_space=pltpu.VMEM)
     log_shape = (count, log_rows, lanes)
     mix_shape = (count, slot_count, rows, LATENT)
-    group_count = slot_sequence.shape[0]
     got_log, got_mix = pl.pallas_call(
         body,
         out_shape=(
@@ -236,7 +236,7 @@
         scratch_shapes=[
             pltpu.VMEM((count, slot_count, rows, key_width), jnp.bfloat16),
             pltpu.VMEM((count, slot_count, rows, key_width), jnp.bfloat16),
-            pltpu.VMEM((slot_count, slab_length, key_width), jnp.bfloat16),
+            pltpu.VMEM((slot_count, key_width, slab_length), jnp.bfloat16),
             pltpu.VMEM(log_shape, jnp.float32),
             pltpu.VMEM(mix_shape, jnp.bfloat16),
             pltpu.SemaphoreType.DMA((slot_count,)),
@@ -251,8 +251,8 @@
         name="attend_slots",
     )(
         context_length,
-        slot_sequence.reshape(group_count, -1),
-        slot_slab.reshape(group_count, -1),
+        slot_sequence,
+        slot_slab,
         every_seq,
         cache_slots,
     )
@@ -333,7 +333,7 @@
     back_log, back_mix = attend_slots(
         1,
         gathered.reshape(group_count * seq_group, DRAFT * heads_here, key_width),
-        kv_cache[0, 0],
+        jnp.swapaxes(kv_cache[0, 0], 1, 2),
         context_length,
         slot_sequence,
         slot_slab,

time: 140 us -> 133 us (0.950)
  local copies, waits for them, and re-layouts: 20.9 us -> 11.1 us
  other arithmetic: 2.48 us -> 4.82 us
    unnamed x19 -> x20, local copies, waits for them, and re-layouts: 15.5 us -> 5.68 us
where the time goes in v3:
time: 133 us; the launch traced here: 132 us
  Pallas kernels  90.3 us (68%)
  matrix products  25.6 us (19%)
  local copies, waits for them, and re-layouts  11.1 us (8%)
  other arithmetic  4.82 us (4%)
    pallas_call x1, Pallas kernels, attend_slots(): pl.pallas_call(body, out_shape=(jax.ShapeDtypeStruct(log_shape, jnp.float...  61.7 us
    pallas_call x3, Pallas kernels, exchange(): pl.pallas_call(body, out_shape=tuple((jax.ShapeDtypeStruct(block.shape, b...  28.6 us
    dot_general x1, matrix products, shards(): partial = jnp.dot(head_values, w_o, preferred_element_type=jnp.float32)  12.3 us
    unnamed x20, local copies, waits for them, and re-layouts  5.68 us
    dot_general x2, matrix products, merge_blocks(): jnp.einsum('sbtx,btxl->stxl', weights, block_out, precision=lax.Precision...  4.96 us
    dot_general x1, matrix products, shards(): jnp.einsum('thn,hnl->thl', q_nope, w_uk, preferred_element_type=jnp.float32)  4.6 us

profile of v3, /device:TPU:1, one launch (start us, length us, event | category | flops | bytes accessed | tf_op | source)
XLA Modules:
  0.0 132.0 jit_solution(4728094897366926223)
XLA Ops:
  0.0 0.6 iota_compare_fusion.1
  0.6 1.0 constant_dynamic-slice_fusion
  2.9 0.7 reshape.196
  3.6 0.7 reshape.192
  4.3 0.8 copy.86.slabs
  5.1 0.8 copy.85.owners
  5.9 1.3 fusion.55
  7.2 0.7 concatenate.22
  7.9 4.6 %convolution_bitcast_fusion.1 = f32[8,16,512]{2,0,1:T(8,128)S(1)} fusion(bf16[16,128,512]{2,1,0:T(8,128)(2,1)} %param.14, bf16[8,1536]{1,0:T(8,128)(2,1)S(1)} %copy-done.5, bf16[1536,2048]{1,0:T(8,128)(2,1)} %param.12), kind=kOutput, calls=%fused_computation.9 | convolution fusion | flops 67125248 | bytes 8675328 | tf_op jit(solution)/shard_map/thn,hnl->thl/dot_general | solution.py:320
  12.7 1.2 fusion.54
  14.0 0.8 fusion.39
  14.8 11.5 %exchange_0.1 = bf16[4,128,576]{2,1,0:T(8,128)(2,1)S(1)} custom-call(bf16[4,128,576]{2,1,0:T(8,128)(2,1)S(1)} %broadcast_in_dim.118.refs_0_), custom_call_target="tpu_custom_call" | custom-call | tf_op jit(solution)/shard_map/exchange_0/pallas_call | solution.py:62
  26.3 2.3 %copy-done.1 = bf16[1,1,2,2048,576]{3,4,2,1,0:T(8,128)(2,1)S(1)} copy-done((bf16[1,1,2,2048,576]{3,4,2,1,0:T(8,128)(2,1)S(1)}, bf16[1,1,2,2048,576]{3,4,2,1,0:T(8,128)(2,1)}, u32[]{:S(2)}) %copy-start.1) | copy-done | bytes 4718616
  28.7 61.7 %attend_slots.1 = (f32[8,8,128]{2,1,0:T(8,128)S(1)}, bf16[8,2,64,512]{3,2,1,0:T(8,128)(2,1)S(1)}) custom-call(s32[8]{0:T(128)S(1)} %copy-done.2, s32[4,8,2]{2,1,0:T(8,128)S(1)} %copy.85.owners, s32[4,8,2]{2,1,0:T(8,128)S(1)} %copy.86.slabs, bf16[8,64,576]{2,1,0:T(8,128)(2,1)S(1)} %bitcast.61, bf16[2,576,2048]{2,1,0:T(8,128)(2,1)S(1)} %bitcast.60), custom_call_target="tpu_custom_call" | custom-call | tf_op jit(solution)/shard_map/attend_slots/pallas_call | solution.py:228
  90.4 1.0 copy-done.3
  92.4 2.4 %fusion.2 = bf16[8,4,16,512]{3,0,2,1:T(8,128)(2,1)S(1)} fusion(bf16[16,4,16,512]{3,2,1,0:T(8,128)(2,1)} %bitcast.63, f32[8,4,16]{0,2,1:T(8,128)S(1)} %get-tuple-element.16, f32[8,4,16]{0,2,1:T(8,128)S(1)} %get-tuple-element.15, f32[8,4,16]{0,2,1:T(8,128)S(1)} %broadcast_maximum_fusion, f32[16,4,16]{0,2,1:T(8,128)S(1)} %copy.87, pred[8,16]{1,0:T(8,128)(4,1)S(1)} %copy-done.6), kind=kOutput, calls=%fused_computation.4 | convolution fusion | flops 51142656 | bytes 1583232 | tf_op jit(solution)/shard_map/sbtx,btxl->stxl/dot_general | solution.py:270
  95.0 9.0 %exchange_3.1 = (f32[4,1,128]{2,1,0:T(1,128)S(1)}, bf16[4,128,512]{2,1,0:T(8,128)(2,1)S(1)}) custom-call(f32[4,1,128]{2,1,0:T(1,128)S(1)} %log_add_fusion.1.refs_0_, bf16[4,128,512]{2,1,0:T(8,128)(2,1)S(1)} %bitcast.62), custom_call_target="tpu_custom_call" | custom-call | tf_op jit(solution)/shard_map/exchange_3/pallas_call | solution.py:62
  103.9 0.8 copy-done.4
  105.2 0.7 reduce.4
  106.4 2.6 %fusion.10 = f32[4,16,512,2]{2,3,1,0:T(2,128)} fusion(bf16[8,4,16,512]{3,2,1,0:T(8,128)(2,1)} %bitcast.64, pred[2,8]{1,0:T(4,128)(4,1)S(1)} %copy-done.7, f32[2,4,16]{0,2,1:T(8,128)S(1)} %copy.95, f32[8,4,16]{0,2,1:T(8,128)S(1)} %copy.92), kind=kOutput, calls=%fused_computation.16 | convolution fusion | flops 6294528 | bytes 789008 | tf_op jit(solution)/shard_map/sbtx,btxl->stxl/dot_general | solution.py:270
  109.4 1.3 fusion.6
  110.7 12.3 %fusion.12 = f32[8,7168]{1,0:T(8,128)S(1)} fusion(bf16[2048,7168]{1,0:T(8,128)(2,1)} %param.16, bf16[16,512,128]{2,1,0:T(8,128)(2,1)} %param.15, bf16[8,16,512]{2,1,0:T(8,128)(2,1)S(1)} %bitcast.67), kind=kOutput, calls=%fused_computation.18 | convolution fusion | flops 251674624 | bytes 31817728 | tf_op jit(solution)/shard_map/dot_general | solution.py:366
  123.1 8.1 %exchange_4.1 = f32[8,1,7168]{2,1,0:T(1,128)S(1)} custom-call(f32[8,1,7168]{2,1,0:T(1,128)S(1)} %reshape.195.refs_0_), custom_call_target="tpu_custom_call" | custom-call | tf_op jit(solution)/shard_map/exchange_4/pallas_call | solution.py:62
  131.2 0.8 reduce_sum.44
  (49 shorter events, 4.4 us)
Async XLA Ops:
  0.0 5.9 %copy-start = (bf16[1536,1024]{1,0:T(8,128)(2,1)S(1)}, bf16[1536,1024]{1,0:T(8,128)(2,1)}, u32[]{:S(2)}) copy-start(bf16[1536,1024]{1,0:T(8,128)(2,1)} %param.13) | copy-start | bytes 9437188
  0.0 7.9 %copy-start.5 = (bf16[8,1536]{1,0:T(8,128)(2,1)S(1)}, bf16[8,1536]{1,0:T(8,128)(2,1)}, u32[]{:S(2)}) copy-start(bf16[8,1536]{1,0:T(8,128)(2,1)} %param.11) | copy-start | bytes 73732
  12.5 13.8 %copy-start.2 = (s32[8]{0:T(128)S(1)}, s32[8]{0:T(128)}, u32[]{:S(2)}) copy-start(s32[8]{0:T(128)} %lengths.1) | copy-start | bytes 100
  14.8 76.8 %copy-start.6 = (pred[8,16]{1,0:T(8,128)(4,1)S(1)}, pred[8,16]{1,0:T(8,128)(4,1)}, u32[]{:S(2)}) copy-start(pred[8,16]{1,0:T(8,128)(4,1)} %iota_compare_fusion) | copy-start | bytes 388
  26.3 2.3 %copy-start.1 = (bf16[1,1,2,2048,576]{3,4,2,1,0:T(8,128)(2,1)S(1)}, bf16[1,1,2,2048,576]{3,4,2,1,0:T(8,128)(2,1)}, u32[]{:S(2)}) copy-start(bf16[1,1,2,2048,576]{3,4,2,1,0:T(8,128)(2,1)} %param.17) | copy-start | bytes 14155780
  90.4 1.0 copy-start.3
  92.4 13.7 %copy-start.7 = (pred[2,8]{1,0:T(4,128)(4,1)S(1)}, pred[2,8]{1,0:T(4,128)(4,1)}, u32[]{:S(2)}) copy-start(pred[2,8]{1,0:T(4,128)(4,1)} %iota_compare_fusion.2) | copy-start | bytes 52
  92.4 17.0 %copy-start.8 = (pred[4,4]{1,0:T(4,128)(4,1)S(1)}, pred[4,4]{1,0:T(4,128)(4,1)}, u32[]{:S(2)}) copy-start(pred[4,4]{1,0:T(4,128)(4,1)} %iota_compare_fusion.1) | copy-start | bytes 52
  103.9 0.8 copy-start.4
